TPU v7x, 512 devices: a whole 4x8x8 slice. The times are simulated.
512 devices in a mesh: tm: 64 (over y, x, z_lo), run: 8 (over z_hi, core).
Axes of the slice: x: 4, y: 8, z: 8 (z_hi: 4, z_lo: 2; z = z_hi * 2 + z_lo), core: 2. Of those that a mesh axis runs over, the one named last changes fastest.
Arguments:
- signal: bfloat16 [8, 65536, 256], P('run', 'tm'), may hold values from -6 to 6
- conv_weight: bfloat16 [768, 512], replicated, may hold values from -0.21875 to 0.21875
- conv_bias: float32 [512], replicated, may hold values from -3 to 3
- out_weight: bfloat16 [256, 256], replicated, may hold values from -0.375 to 0.375
- out_bias: float32 [256], replicated, may hold values from -3 to 3
- cotangent: bfloat16 [8, 65536, 256], P('run', 'tm'), may hold values from -8 to 8
Outputs:
- output: bfloat16 [8, 65536, 256], P('run', 'tm')
- grad_signal: bfloat16 [8, 65536, 256], P('run', 'tm')
- grad_conv_weight: float32 [768, 512], replicated
- grad_conv_bias: float32 [512], replicated
- grad_out_weight: float32 [256, 256], replicated
- grad_out_bias: float32 [256], replicated
All inputs are finite; a program needn't handle non-finite values.
Results may differ from a plain program's by a relative error of at most 0.0034.
Values may be sent and summed in bfloat16 or wider, within the bound.
A program may use at most 64 MiB of HBM per device.

v0:
```python
import jax
import jax.numpy as jnp
from jax import lax
from jax.sharding import PartitionSpec as P

DILATION_STEPS = 256
KERNEL_TAPS = 3


def passed_along(array, axis, by):
    size = lax.axis_size(axis)
    pairs = [(i, i + by) for i in range(size) if 0 <= i + by < size]
    return lax.ppermute(array, axis, pairs)


def local(signal, conv_weight, conv_bias, out_weight, out_bias, cotangent):
    device_rows = signal.shape[1]
    channels = signal.shape[2]
    receptive_span = (KERNEL_TAPS - 1) * DILATION_STEPS
    history = passed_along(signal[:, device_rows - receptive_span :, :], "tm", 1)
    padded_input = jnp.concatenate([history, signal], 1)
    tap_stack = jnp.concatenate(
        [
            padded_input[
                :,
                receptive_span
                - kernel_tap_index * DILATION_STEPS : receptive_span
                - kernel_tap_index * DILATION_STEPS
                + device_rows,
            ]
            for kernel_tap_index in range(KERNEL_TAPS)
        ],
        2,
    )
    preact = (
        jnp.einsum("bsk,kn->bsn", tap_stack, conv_weight, preferred_element_type=jnp.float32)
        + conv_bias
    )
    filtered = jnp.tanh(preact[..., :channels])
    gated = jax.nn.sigmoid(preact[..., channels:])
    mixed = (filtered * gated).astype(jnp.bfloat16)
    hidden = (
        jnp.einsum("bsc,cd->bsd", mixed, out_weight, preferred_element_type=jnp.float32) + out_bias
    )
    output = (signal.astype(jnp.float32) + hidden).astype(jnp.bfloat16)
    dmixed = jnp.einsum("bsd,cd->bsc", cotangent, out_weight, preferred_element_type=jnp.float32)
    dpre = jnp.concatenate(
        [dmixed * gated * (1.0 - filtered * filtered), dmixed * filtered * gated * (1.0 - gated)], 2
    ).astype(jnp.bfloat16)
    dstacked = jnp.einsum("bsn,kn->bsk", dpre, conv_weight, preferred_element_type=jnp.float32)
    local_grad = jnp.zeros((signal.shape[0], receptive_span + device_rows, channels), jnp.float32)
    for kernel_tap_index in range(KERNEL_TAPS):
        shifted_slice = dstacked[
            ..., kernel_tap_index * channels : (kernel_tap_index + 1) * channels
        ]
        local_grad = local_grad + jnp.pad(
            shifted_slice,
            (
                (0, 0),
                (
                    receptive_span - kernel_tap_index * DILATION_STEPS,
                    kernel_tap_index * DILATION_STEPS,
                ),
                (0, 0),
            ),
        )
    incoming = passed_along(local_grad[:, :receptive_span].astype(jnp.bfloat16), "tm", -1).astype(
        jnp.float32
    )
    grad_signal = (
        cotangent.astype(jnp.float32)
        + local_grad[:, receptive_span:]
        + jnp.pad(incoming, ((0, 0), (device_rows - receptive_span, 0), (0, 0)))
    )
    grad_signal = grad_signal.astype(jnp.bfloat16)
    grad_conv = jnp.einsum("bsk,bsn->kn", tap_stack, dpre, preferred_element_type=jnp.float32)
    grad_cbias = jnp.sum(dpre.astype(jnp.float32), (0, 1))
    grad_proj = jnp.einsum("bsc,bsd->cd", mixed, cotangent, preferred_element_type=jnp.float32)
    grad_pbias = jnp.sum(cotangent.astype(jnp.float32), (0, 1))
    scale = float(signal.shape[0] * lax.axis_size("run") * device_rows * lax.axis_size("tm")) ** (
        -0.5
    )
    summed = lax.psum((grad_conv, grad_cbias, grad_proj, grad_pbias), ("tm", "run"))
    return (
        output,
        grad_signal,
        summed[0] * scale,
        summed[1] * scale,
        summed[2] * scale,
        summed[3] * scale,
    )


def solution(mesh):
    placed = (P("run", "tm", None), P(), P(), P(), P(), P("run", "tm", None))
    return jax.shard_map(
        local,
        mesh=mesh,
        in_specs=placed,
        out_specs=(P("run", "tm", None), P("run", "tm", None), P(), P(), P(), P()),
        check_vma=False,
    )
```

profile of v0, /device:TPU:1, one launch (start us, length us, event | category | flops | bytes accessed | tf_op | source)
XLA Modules:
  0.0 329.9 jit_solution(11281328637928422365)
XLA Ops:
  7.2 0.0 copy-start
  7.2 0.0 copy-start.2
  7.2 0.0 all-reduce.8.cloned.1.call-start
  7.2 1.1 slice.31
  8.3 4.8 %collective-permute-start = (bf16[1,512,256]{2,1,0:T(8,128)(2,1)S(1)}, bf16[1,512,256]{2,1,0:T(8,128)(2,1)S(1)}, u32[]{:S(2)}, u32[]{:S(2)}) collective-permute-start(bf16[1,512,256]{2,1,0:T(8,128)(2,1)S(1)} %slice.31), channel_id=1, source_target_pairs={{0,8},{8,16},{16,24},{24,32},{32,40},{40,48},{48,56},{56,64},{64,7... | collective-permute-start | bytes 786440 | tf_op jit(solution)/shard_map/ppermute | solution.py:13
  13.2 3.3 collective-permute-done
  16.5 1.1 constant_dynamic-update-slice_fusion
  17.5 0.1 fusion.17
  17.7 0.0 copy-start.1
  17.7 0.0 copy-start.5
  17.7 1.0 add_bitcast_fusion
  18.7 0.8 multiply_convert_fusion.1
  19.5 0.0 copy-start.3
  19.5 0.2 convert_reduce_fusion
  19.8 2.2 fusion.8
  21.9 2.7 convolution_bitcast_fusion
  24.6 1.0 fusion.10
  25.6 2.1 fusion.16
  27.7 0.2 pad_add_fusion
  27.9 0.0 copy-start.7
  27.9 0.7 slice.74
  28.7 1.3 collective-permute-start.1
  30.0 0.0 all-reduce.8.cloned.1.call-update
  30.0 2.2 fusion.2
  32.2 4.4 %collective-permute-done.1 = bf16[1,512,256]{2,1,0:T(8,128)(2,1)} collective-permute-done((bf16[1,512,256]{2,1,0:T(8,128)(2,1)}, bf16[1,512,256]{2,1,0:T(8,128)(2,1)}, u32[]{:S(2)}, u32[]{:S(2)}) %collective-permute-start.1) | collective-permute-done | bytes 262176 | tf_op jit(solution)/shard_map/ppermute | solution.py:13
  36.6 2.0 convert_reduce_fusion.1
  38.6 113.1 %all-reduce.4 = (f32[512]{0:T(512)S(1)}, f32[256]{0:T(256)S(1)}) all-reduce(f32[512]{0:T(512)S(1)} %convert_reduce_fusion, f32[256]{0:T(256)S(1)} %get-tuple-element.18), channel_id=1, replica_groups=mesh['tm'=64,'run'=8] {'tm','run'}, use_global_device_ids=true, to_apply=%region_2.3 | all-reduce | flops 768 | bytes 6144 | tf_op jit(solution)/shard_map/psum | solution.py:83
  151.6 0.6 broadcast_multiply_fusion.3
  152.2 0.6 broadcast_multiply_fusion.2
  152.8 166.8 %all-reduce.8.cloned.1.call-done = (f32[768,512]{1,0:T(8,128)}, f32[256,256]{1,0:T(8,128)}) async-done(((f32[768,512]{1,0:T(8,128)}, f32[256,256]{1,0:T(8,128)}), (f32[768,512]{1,0:T(8,128)}, f32[256,256]{1,0:T(8,128)})) %all-reduce.8.cloned.1.call-update) | async-done | bytes 1835024 | tf_op jit(solution)/shard_map/psum | solution.py:83
  319.5 2.8 broadcast_multiply_fusion
  322.3 0.7 broadcast_multiply_fusion.1
  (11 shorter events, 0.0 us)
Async XLA Ops:
  7.2 10.5 %copy-start = (bf16[768,512]{1,0:T(8,128)(2,1)S(1)}, bf16[768,512]{1,0:T(8,128)(2,1)}, u32[]{:S(2)}) copy-start(bf16[768,512]{1,0:T(8,128)(2,1)} %param.7) | copy-start | bytes 2359300
  7.2 10.5 %copy-start.2 = (bf16[1,1024,256]{2,1,0:T(8,128)(2,1)S(1)}, bf16[1,1024,256]{2,1,0:T(8,128)(2,1)}, u32[]{:S(2)}) copy-start(bf16[1,1024,256]{2,1,0:T(8,128)(2,1)} %param.6) | copy-start | bytes 1572868
  7.2 10.5 %copy-start.6 = (f32[512]{0:T(512)S(1)}, f32[512]{0:T(512)}, u32[]{:S(2)}) copy-start(f32[512]{0:T(512)} %param.8) | copy-start | bytes 6148
  7.2 312.3 %all-reduce.8.cloned.1.call-start = ((), (), s32[]{:S(2)}) async-start(), calls=%async_computation | async-start | bytes 3670016 | tf_op jit(solution)/shard_map/psum | solution.py:83
  8.3 8.1 %collective-permute-start = (bf16[1,512,256]{2,1,0:T(8,128)(2,1)S(1)}, bf16[1,512,256]{2,1,0:T(8,128)(2,1)S(1)}, u32[]{:S(2)}, u32[]{:S(2)}) collective-permute-start(bf16[1,512,256]{2,1,0:T(8,128)(2,1)S(1)} %slice.31), channel_id=1, source_target_pairs={{0,8},{8,16},{16,24},{24,32},{32,40},{40,48},{48,56},{56,64},{64,7... | collective-permute-start | bytes 786440 | tf_op jit(solution)/shard_map/ppermute | solution.py:13
  17.7 1.1 copy-start.1
  17.7 1.1 copy-start.5
  19.5 5.1 %copy-start.3 = (bf16[1024,256]{0,1:T(8,128)(2,1)}, bf16[1024,256]{0,1:T(8,128)(2,1)S(1)}, u32[]{:S(2)}) copy-start(bf16[1024,256]{0,1:T(8,128)(2,1)S(1)} %get-tuple-element.15) | copy-start | bytes 1572868
  27.9 2.1 copy-start.7
  28.7 7.9 %collective-permute-start.1 = (bf16[1,512,256]{2,1,0:T(8,128)(2,1)}, bf16[1,512,256]{2,1,0:T(8,128)(2,1)}, u32[]{:S(2)}, u32[]{:S(2)}) collective-permute-start(bf16[1,512,256]{2,1,0:T(8,128)(2,1)} %slice.74), channel_id=1, source_target_pairs={{8,0},{16,8},{24,16},{32,24},{40,32},{48,40},{56,48},{64,56},{72,6... | collective-permute-start | bytes 786440 | tf_op jit(solution)/shard_map/ppermute | solution.py:13
  319.5 2.8 copy-start.4
Sparse Core Ops, SparseCore 0:
  30.1 289.3 all-reduce.7
where the time goes:
time: 330 us
  waiting for transfers between devices  174 us (53%)
  blocking collectives  113 us (34%)
  between operations  14.2 us (4%)
  matrix products  9.89 us (3%)
  other arithmetic  7.02 us (2%)
  starting transfers between devices  6.16 us (2%)
  local copies, waits for them, and re-layouts  5.08 us (2%)
    psum x1, waiting for transfers between devices, local(): lax.psum((grad_conv, grad_cbias, grad_proj, grad_pbias), ('tm', 'run'))  167 us
    psum x1, blocking collectives, local(): lax.psum((grad_conv, grad_cbias, grad_proj, grad_pbias), ('tm', 'run'))  113 us
    ppermute x2, waiting for transfers between devices, passed_along(): return lax.ppermute(array, axis, pairs)  7.68 us
  transfers between devices with their start and end apart: 3, of which 3 were waited for; matrix products, arithmetic and copies ran while one was open for 2% of the time, Pallas kernels for 0%

commit v1 on v0

--- a/solution.py
+++ b/solution.py
@@ -80,7 +80,9 @@
     scale = float(signal.shape[0] * lax.axis_size("run") * device_rows * lax.axis_size("tm")) ** (
         -0.5
     )
-    summed = lax.psum((grad_conv, grad_cbias, grad_proj, grad_pbias), ("tm", "run"))
+    summed = (grad_conv, grad_cbias, grad_proj, grad_pbias)
+    for over in ("run", "tm"):
+        summed = lax.psum(summed, over)
     return (
         output,
         grad_signal,

time: 330 us -> 738 us (2.24)
  the two profiles are of different devices: /device:TPU:1 before, /device:TPU:30 now
where the time goes in v1:
time: 738 us
  waiting for transfers between devices  530 us (72%)
  blocking collectives  171 us (23%)
  between operations  14.2 us (2%)
  starting transfers between devices  7.53 us (1%)
    psum x2, waiting for transfers between devices, local(): summed = lax.psum(summed, over)  519 us
    psum x2, blocking collectives, local(): summed = lax.psum(summed, over)  171 us
  transfers between devices with their start and end apart: 4, of which 4 were waited for; matrix products, arithmetic and copies ran while one was open for 1% of the time, Pallas kernels for 0%

profile of v1, /device:TPU:30, one launch (start us, length us, event | category | flops | bytes accessed | tf_op | source)
XLA Modules:
  0.0 738.0 jit_solution(1374340505601241953)
XLA Ops:
  7.2 0.0 copy-start
  7.2 0.0 all-reduce.13.cloned.1.call-start
  7.3 1.1 slice.31
  8.3 4.3 collective-permute-start
  12.6 6.6 collective-permute-done
  19.2 1.1 constant_dynamic-update-slice_fusion
  20.3 0.1 fusion.17
  20.4 0.0 copy-start.4
  20.4 1.0 add_bitcast_fusion
  21.5 0.8 multiply_convert_fusion.1
  22.2 1.0 fusion.10
  23.2 2.2 fusion.8
  25.4 0.0 all-reduce.13.cloned.1.call-update
  25.4 0.0 all-reduce.11.cloned.1.call-start
  25.5 94.2 %all-reduce.13.cloned.1.call-done = (f32[768,512]{1,0:T(8,128)}, f32[256,256]{1,0:T(8,128)}) async-done(((f32[768,512]{1,0:T(8,128)}, f32[256,256]{1,0:T(8,128)}), (f32[768,512]{1,0:T(8,128)}, f32[256,256]{1,0:T(8,128)})) %all-reduce.13.cloned.1.call-update) | async-done | bytes 1835024 | tf_op jit(solution)/shard_map/psum | solution.py:85
  119.7 0.0 all-reduce.11.cloned.1.call-update
  119.7 1.0 convolution_bitcast_fusion
  120.8 0.3 fusion.16
  121.1 0.0 copy-start.6
  121.1 0.2 pad_add_fusion
  121.4 3.2 collective-permute-start.1
  124.5 0.2 convert_reduce_fusion
  124.8 1.2 fusion.2
  125.9 4.4 collective-permute-done.1
  130.3 1.1 convert_reduce_fusion.1
  131.4 16.2 %all-reduce.6 = (f32[512]{0:T(512)S(1)}, f32[256]{0:T(256)S(1)}) all-reduce(f32[512]{0:T(512)S(1)} %convert_reduce_fusion, f32[256]{0:T(256)S(1)} %get-tuple-element.22), channel_id=1, replica_groups=mesh['tm'=64,'run'=8] {'run'}, use_global_device_ids=true, to_apply=%region_3.4 | all-reduce | flops 768 | bytes 6144 | tf_op jit(solution)/shard_map/psum | solution.py:85
  147.6 154.5 %all-reduce.4 = (f32[512]{0:T(512)S(1)}, f32[256]{0:T(256)S(1)}) all-reduce(f32[512]{0:T(512)S(1)} %get-tuple-element.10, f32[256]{0:T(256)S(1)} %get-tuple-element.11), channel_id=1, replica_groups=mesh['tm'=64,'run'=8] {'tm'}, use_global_device_ids=true, to_apply=%region_4.5 | all-reduce | flops 768 | bytes 6144 | tf_op jit(solution)/shard_map/psum | solution.py:85
  302.1 0.6 broadcast_multiply_fusion.3
  302.7 0.6 broadcast_multiply_fusion.2
  303.2 424.4 %all-reduce.11.cloned.1.call-done = (f32[768,512]{1,0:T(8,128)}, f32[256,256]{1,0:T(8,128)}) async-done(((f32[768,512]{1,0:T(8,128)}, f32[256,256]{1,0:T(8,128)}), (f32[768,512]{1,0:T(8,128)}, f32[256,256]{1,0:T(8,128)})) %all-reduce.11.cloned.1.call-update) | async-done | bytes 1835024 | tf_op jit(solution)/shard_map/psum | solution.py:85
  727.7 2.8 broadcast_multiply_fusion
  730.4 0.7 broadcast_multiply_fusion.1
  (13 shorter events, 0.1 us)
Async XLA Ops:
  7.2 13.2 %copy-start = (bf16[768,512]{1,0:T(8,128)(2,1)S(1)}, bf16[768,512]{1,0:T(8,128)(2,1)}, u32[]{:S(2)}) copy-start(bf16[768,512]{1,0:T(8,128)(2,1)} %param.7) | copy-start | bytes 2359300
  7.2 13.2 %copy-start.2 = (bf16[1,1024,256]{2,1,0:T(8,128)(2,1)S(1)}, bf16[1,1024,256]{2,1,0:T(8,128)(2,1)}, u32[]{:S(2)}) copy-start(bf16[1,1024,256]{2,1,0:T(8,128)(2,1)} %param.6) | copy-start | bytes 1572868
  7.2 13.2 %copy-start.5 = (f32[512]{0:T(512)S(1)}, f32[512]{0:T(512)}, u32[]{:S(2)}) copy-start(f32[512]{0:T(512)} %param.8) | copy-start | bytes 6148
  7.2 112.5 %all-reduce.13.cloned.1.call-start = ((), (), s32[]{:S(2)}) async-start(), calls=%async_computation.1 | async-start | bytes 3670016 | tf_op jit(solution)/shard_map/psum | solution.py:85
  8.3 10.8 %collective-permute-start = (bf16[1,512,256]{2,1,0:T(8,128)(2,1)S(1)}, bf16[1,512,256]{2,1,0:T(8,128)(2,1)S(1)}, u32[]{:S(2)}, u32[]{:S(2)}) collective-permute-start(bf16[1,512,256]{2,1,0:T(8,128)(2,1)S(1)} %slice.31), channel_id=1, source_target_pairs={{0,8},{8,16},{16,24},{24,32},{32,40},{40,48},{48,56},{56,64},{64,7... | collective-permute-start | bytes 786440 | tf_op jit(solution)/shard_map/ppermute | solution.py:13
  20.4 1.1 copy-start.1
  20.4 1.1 copy-start.4
  25.4 702.2 %all-reduce.11.cloned.1.call-start = ((), (), s32[]{:S(2)}) async-start(), calls=%async_computation | async-start | bytes 3670016 | tf_op jit(solution)/shard_map/psum | solution.py:85
  121.1 3.7 copy-start.6
  121.4 9.0 %collective-permute-start.1 = (bf16[1,512,256]{2,1,0:T(8,128)(2,1)S(1)}, bf16[1,512,256]{2,1,0:T(8,128)(2,1)S(1)}, u32[]{:S(2)}, u32[]{:S(2)}) collective-permute-start(bf16[1,512,256]{2,1,0:T(8,128)(2,1)S(1)} %slice.74), channel_id=1, source_target_pairs={{8,0},{16,8},{24,16},{32,24},{40,32},{48,40},{56,48},{64,56},{72,6... | collective-permute-start | bytes 786440 | tf_op jit(solution)/shard_map/ppermute | solution.py:13
  727.7 2.8 copy-start.3
Sparse Core Ops, SparseCore 0:
  25.6 94.0 all-reduce.12
  122.7 604.9 all-reduce.10
